TPU v7x, 256 devices: a whole 4x4x8 slice. The times are simulated.
256 devices in a mesh: scen: 16 (over x, z_lo), link: 16 (over z_hi, y, core).
Axes of the slice: x: 4, y: 4, z: 8 (z_hi: 2, z_lo: 4; z = z_hi * 4 + z_lo), core: 2. Of those that a mesh axis runs over, the one named last changes fastest.
Arguments:
- link_rows: bfloat16 [192, 2048, 4096], P('scen', None, 'link'), may hold values from -1 to 1
- slot_scenario: int32 [192, 16], P('scen'), may hold values from 0 to 162, as said below
- diag_scaling: float32 [2592, 2048], P('scen'), may hold values from 0.1 to 10
- regulariser: float32 [4096], P('link'), may hold values from 0.125 to 1
- right_side: float32 [4096], P('link'), may hold values from -6 to 6
Outputs:
- direction: float32 [4096], P('link')
- scenario_step: float32 [2592, 2048], P('scen', 'link')
Inputs may be any that keep to these rules, and one draw needn't show every extreme that they name: `slot_scenario`: values of 162 mark empty slots. A scenario occupies at most one slot of a tile, and its tiles are one tile or two neighbouring tiles. In every block some tile has all 12 slots live, and at most 1 scenario of a block touches both of two neighbouring tiles; some pair of neighbouring tiles of every block reaches that number.
All inputs are finite; a program needn't handle non-finite values.
Results may differ from a plain program's by a relative error of at most 0.0029.
The roundings to bfloat16 on the way count: a program that leaves them out, or rounds other values in their place, can miss the bound.
Values may be sent and summed in bfloat16 or wider, within the bound.
A program may use at most 128 MiB of HBM per device.

v0:
```python
import jax
import jax.numpy as jnp
from jax import lax
from jax.sharding import PartitionSpec as P

CAP2 = 1
SWEEPS = 2


def shifted(shard, axis, by):
    count = lax.axis_size(axis)
    pairs = [(i, i + by) for i in range(count) if 0 <= i + by < count]
    return lax.ppermute(shard, axis, pairs)


def extended(block, sides, width):
    for axis, dim in sides:
        count = lax.axis_size(axis)
        forward = [(i, i + 1) for i in range(count - 1)]
        backward = [(target, source) for source, target in forward]
        low = lax.ppermute(
            lax.slice_in_dim(block, block.shape[dim] - width, None, axis=dim), axis, forward
        )
        high = lax.ppermute(lax.slice_in_dim(block, 0, width, axis=dim), axis, backward)
        block = jnp.concatenate([low, block, high], axis=dim)
    return block


def straddle_select(low_ids, high_ids, allowed, scen_count, straddle_cap):
    matches = (low_ids[:, None] == high_ids[None, :]) & (low_ids[:, None] < scen_count) & allowed
    flagged = jnp.any(matches, axis=1)
    order_pos = jnp.cumsum(flagged.astype(jnp.int32)) - 1
    wanted = jnp.arange(straddle_cap, dtype=jnp.int32)
    picker = flagged[None, :] & (order_pos[None, :] == wanted[:, None])
    low_pick = picker.astype(jnp.float32)
    high_pick = jnp.dot(low_pick, matches.astype(jnp.float32), precision=lax.Precision.HIGHEST)
    return (low_pick, high_pick)


def chol_apply(factor, vector):
    column = vector[:, None]
    inner = lax.linalg.triangular_solve(factor, column, left_side=True, lower=True)
    outer = lax.linalg.triangular_solve(factor, inner, left_side=True, lower=True, transpose_a=True)
    return outer[:, 0]


def contract_slots(left, right):
    return lax.dot_general(
        left, right, (((0, 1), (0, 1)), ((), ())), preferred_element_type=jnp.float32
    )


def shards(link_rows, slot_scenario, diag_scaling, regulariser, right_side):
    slot_cap, width, tile_rows = link_rows.shape
    tile_count = slot_scenario.shape[1]
    scen_count = diag_scaling.shape[0]
    tile_index = lax.axis_index("link")
    next_index = jnp.minimum(tile_index + 1, tile_count - 1)
    prev_index = jnp.maximum(tile_index - 1, 0)
    ids_here = lax.dynamic_index_in_dim(slot_scenario, tile_index, 1, False)
    ids_next = lax.dynamic_index_in_dim(slot_scenario, next_index, 1, False)
    ids_prev = lax.dynamic_index_in_dim(slot_scenario, prev_index, 1, False)
    live = ids_here < scen_count
    slot_scale = jnp.take(diag_scaling, jnp.minimum(ids_here, scen_count - 1), axis=0)
    slot_scale = jnp.where(live[:, None], slot_scale, jnp.float32(0.0))
    scaled = (link_rows * slot_scale[:, :, None]).astype(jnp.bfloat16)
    diag_part = contract_slots(scaled, link_rows)
    up_low, unused_high = straddle_select(
        ids_here, ids_next, tile_index + 1 < tile_count, scen_count, CAP2
    )
    unused_low, down_high = straddle_select(ids_prev, ids_here, tile_index > 0, scen_count, CAP2)
    own_up = jnp.einsum(
        "jc,cnr->jnr", up_low.astype(jnp.bfloat16), scaled, preferred_element_type=jnp.float32
    ).astype(jnp.bfloat16)
    own_down = jnp.einsum(
        "jc,cnr->jnr", down_high.astype(jnp.bfloat16), link_rows, preferred_element_type=jnp.float32
    ).astype(jnp.bfloat16)
    from_next = shifted(own_down, "link", -1)
    upper_part = contract_slots(own_up, from_next)
    diag_sum, upper_sum = lax.psum((diag_part, upper_part), "scen")
    lower_sum = shifted(upper_sum, "link", 1).T
    schur_diag = diag_sum + jnp.diag(regulariser)
    factor = jnp.linalg.cholesky(schur_diag)
    colour_here = tile_index % 2
    current = jnp.where(
        colour_here == 0, chol_apply(factor, right_side), jnp.zeros_like(right_side)
    )
    for half_step in range(2 * SWEEPS - 1):
        colour = (half_step + 1) % 2
        beside_all = extended(current[None, :], (("link", 0),), 1)
        coupled = jnp.dot(lower_sum, beside_all[0], precision=lax.Precision.HIGHEST) + jnp.dot(
            upper_sum, beside_all[2], precision=lax.Precision.HIGHEST
        )
        current = jnp.where(
            colour_here == colour, chol_apply(factor, right_side - coupled), current
        )
    half_dir = current.astype(jnp.bfloat16)
    slot_values = jnp.einsum("cnr,r->cn", link_rows, half_dir, preferred_element_type=jnp.float32)
    column_piece = width // lax.axis_size("link")
    columns = lax.dynamic_slice_in_dim(diag_scaling, tile_index * column_piece, column_piece, 1)
    scen_ids = jnp.arange(scen_count, dtype=jnp.int32)
    picker = (scen_ids[:, None] == ids_here[None, :]).astype(jnp.float32)
    partial_terms = jnp.dot(picker, slot_values, precision=lax.Precision.HIGHEST)
    summed = lax.psum_scatter(partial_terms, "link", scatter_dimension=1, tiled=True)
    return (current, columns * summed)


def solution(mesh):
    in_specs = (P("scen", None, "link"), P("scen", None), P("scen", None), P("link"), P("link"))
    out_specs = (P("link"), P("scen", "link"))
    return jax.shard_map(shards, mesh=mesh, in_specs=in_specs, out_specs=out_specs, check_vma=False)
```

profile of v0, /device:TPU:1, one launch (start us, length us, event | category | flops | bytes accessed | tf_op | source)
XLA Modules:
  0.0 440.6 jit_solution(11184617385202656466)
XLA Ops:
  7.2 1.0 dynamic-slice_reduce_fusion
  9.0 12.2 %fusion = bf16[1,2048,256]{2,0,1:T(2,128)(2,1)S(1)} fusion(bf16[12,1,1]{0,1,2:T(2,128)(2,1)S(1)} %fusion.15, bf16[12,2048,256]{2,1,0:T(8,128)(2,1)} %param.9), kind=kOutput, calls=%fused_computation.4 | convolution fusion | flops 12582912 | bytes 13631512 | tf_op jit(solution)/shard_map/jc,cnr->jnr/dot_general | solution.py:75
  21.4 5.3 %collective-permute-start = (bf16[1,2048,256]{2,1,0:T(8,128)(2,1)S(1)}, bf16[1,2048,256]{2,1,0:T(8,128)(2,1)S(1)}, u32[]{:S(2)}, u32[]{:S(2)}) collective-permute-start(bf16[1,2048,256]{2,1,0:T(8,128)(2,1)S(1)} %copy.79), channel_id=1, source_target_pairs={{1,0},{2,1},{3,2},{4,3},{5,4},{6,5},{7,6},{8,7},{9,8},{10,9},{11,1... | collective-permute-start | bytes 3145736 | tf_op jit(solution)/shard_map/ppermute | solution.py:13
  26.7 1.2 gather_fusion
  28.0 1.0 select_select_fusion.1
  29.0 12.4 %fusion.5 = f32[256,256]{0,1:T(8,128)} fusion(bf16[12,2048,256]{2,1,0:T(8,128)(2,1)} %param.9, f32[12,2048]{1,0:T(8,128)S(1)} %select_select_fusion.1), kind=kOutput, calls=%fused_computation.11 | convolution fusion | flops 3240099840 | bytes 12943360 | tf_op jit(solution)/shard_map/dot_general | solution.py:48
  41.3 11.6 %multiply_convert_fusion = bf16[12,2048,256]{2,1,0:T(8,128)(2,1)} fusion(bf16[12,2048,256]{2,1,0:T(8,128)(2,1)} %param.9, f32[12,2048]{1,0:T(8,128)S(1)} %select_select_fusion.1), kind=kLoop, calls=%fused_computation.3 | loop fusion | flops 18874368 | bytes 25264128 | tf_op jit(solution)/shard_map/convert_element_type | solution.py:66
  53.2 12.2 %fusion.2 = bf16[1,2048,256]{2,0,1:T(2,128)(2,1)S(1)} fusion(bf16[12,2048,256]{2,1,0:T(8,128)(2,1)} %multiply_convert_fusion, pred[12]{0:T(512)(128)(4,1)S(1)} %get-tuple-element.161, s32[12,1]{0,1:T(1,128)S(1)} %reduce-window.18), kind=kOutput, calls=%fused_computation.6 | convolution fusion | flops 12582972 | bytes 13631548 | tf_op jit(solution)/shard_map/jc,cnr->jnr/dot_general | solution.py:72
  65.4 1.2 fusion.16
  66.6 0.3 reduce-scatter.2.cloned.1.call-start
  66.9 153.0 %all-reduce.4.cloned.1.call-done = (f32[256,256]{0,1:T(8,128)}, f32[256,256]{1,0:T(8,128)}) async-done(((f32[256,256]{0,1:T(8,128)}, f32[256,256]{1,0:T(8,128)}), (f32[256,256]{0,1:T(8,128)}, f32[256,256]{1,0:T(8,128)})) %all-reduce.4.cloned.1.call-update) | async-done | bytes 524304 | tf_op jit(solution)/shard_map/psum | solution.py:80
  219.9 1.0 select_add_fusion
  221.0 1.0 fusion.25
  222.0 11.7 %cholesky.49 = f32[128,128]{1,0:T(8,128)S(1)} custom-call(f32[128,128]{1,0:T(8,128)S(1)} %cholesky.115), custom_call_target="Cholesky" | custom-call | tf_op jit(solution)/shard_map/jit(cholesky)/cholesky | solution.py:83
  233.8 9.8 %custom-call.17 = f32[1,128,128]{1,2,0:T(8,128)S(1)} custom-call(f32[1,128,128]{2,1,0:T(8,128)S(1)} %get-tuple-element.175), custom_call_target="InvertDiagBlocksLowerTriangular" | custom-call | tf_op jit(solution)/shard_map/jit(cholesky)/cholesky | solution.py:83
  243.8 0.3 convolution_subtract_fusion
  244.1 11.7 %cholesky.103 = f32[128,128]{1,0:T(8,128)S(1)} custom-call(f32[128,128]{1,0:T(8,128)S(1)} %convolution_subtract_fusion), custom_call_target="Cholesky" | custom-call | tf_op jit(solution)/shard_map/jit(cholesky)/cholesky | solution.py:83
  256.1 0.7 compare_reduce_fusion
  256.8 0.6 compare_reduce_fusion.1
  258.9 4.4 %while.16 = (s32[]{:T(128)}, f32[256,256]{0,1:T(8,128)S(1)}, s32[2,2]{1,0:T(2,128)S(1)}, f32[2,128,128]{2,1,0:T(8,128)S(1)}, s32[]{:T(128)}) while((s32[]{:T(128)}, f32[256,256]{0,1:T(8,128)S(1)}, s32[2,2]{1,0:T(2,128)S(1)}, f32[2,128,128]{2,1,0:T(8,128)S(1)}, s32[]{:T(128)}) %tuple.78), condition=%wide.while_cond.1.clone.2, body=%wide.while_body.1.clone.2.sunk | while | flops 2 | bytes 393321 | solution.py:43
  259.2 0.6 fusion.110
  259.7 1.4 dynamic-slice.22
  261.2 0.6 fusion.110
  261.8 1.4 dynamic-slice.22
  263.3 19.7 %custom-call.31 = f32[2,128,128]{1,2,0:T(8,128)S(1)} custom-call(f32[2,128,128]{2,1,0:T(8,128)S(1)} %get-tuple-element.63), custom_call_target="InvertDiagBlocksLowerTriangular" | custom-call | tf_op jit(solution)/shard_map/triangular_solve/custom-call.4 | solution.py:43
  283.7 0.2 fusion.12
  283.9 0.2 convolution_bitcast_fusion.18
  284.1 13.9 %collective-permute-start.1 = (f32[256,256]{1,0:T(8,128)}, f32[256,256]{1,0:T(8,128)S(1)}, u32[]{:S(2)}, u32[]{:S(2)}) collective-permute-start(f32[256,256]{1,0:T(8,128)} %get-tuple-element.171), channel_id=1, source_target_pairs={{0,1},{1,2},{2,3},{3,4},{4,5},{5,6},{6,7},{7,8},{8,9},{9,10},{10,1... | collective-permute-start | bytes 786440 | tf_op jit(solution)/shard_map/ppermute | solution.py:13
  298.1 1.9 collective-permute-start.3
  300.0 3.6 collective-permute-start.2
  303.7 1.2 fusion.56
  305.9 0.2 fusion.10
  306.1 0.2 convolution_bitcast_fusion.12
  306.4 1.9 collective-permute-start.5
  308.3 3.6 collective-permute-start.4
  312.0 1.2 fusion.53
  313.3 0.2 fusion.21
  314.2 0.2 fusion.8
  314.5 0.2 convolution_bitcast_fusion.6
  314.7 1.9 collective-permute-start.7
  316.7 3.6 collective-permute-start.6
  320.3 1.2 fusion.50
  322.6 0.2 fusion.6
  322.8 0.2 convolution_bitcast_fusion
  323.1 7.9 %fusion.79 = f32[1,12,2048]{2,0,1:T(1,128)S(1)} fusion(bf16[256,1,1]{0,1,2:T(2,128)(2,1)S(1)} %reshape.483, bf16[12,2048,256]{2,1,0:T(8,128)(2,1)} %param.9), kind=kOutput, calls=%fused_computation.154 | convolution fusion | flops 12582912 | bytes 12681728 | tf_op jit(solution)/shard_map/cnr,r->cn/dot_general | solution.py:98
  331.0 1.8 fusion.26
  332.8 98.9 %reduce-scatter.2.cloned.1.call-done = f32[162,128]{1,0:T(8,128)} async-done(((f32[162,2048]{1,0:T(8,128)}), f32[162,128]{1,0:T(8,128)}) %reduce-scatter.2.cloned.1.call-update) | async-done | bytes 82960 | tf_op jit(solution)/shard_map/reduce_scatter | solution.py:104
  431.8 1.5 dynamic-slice_multiply_fusion
  (79 shorter events, 5.7 us)
Async XLA Ops:
  7.2 19.6 %copy-start = (f32[162,2048]{1,0:T(8,128)S(1)}, f32[162,2048]{1,0:T(8,128)}, u32[]{:S(2)}) copy-start(f32[162,2048]{1,0:T(8,128)} %param.11) | copy-start | bytes 3981316
  7.2 212.7 %all-reduce.4.cloned.1.call-start = ((), (), s32[]{:S(2)}) async-start(), calls=%async_computation.2 | async-start | bytes 1048576 | tf_op jit(solution)/shard_map/psum | solution.py:80
  21.4 43.9 %collective-permute-start = (bf16[1,2048,256]{2,1,0:T(8,128)(2,1)S(1)}, bf16[1,2048,256]{2,1,0:T(8,128)(2,1)S(1)}, u32[]{:S(2)}, u32[]{:S(2)}) collective-permute-start(bf16[1,2048,256]{2,1,0:T(8,128)(2,1)S(1)} %copy.79), channel_id=1, source_target_pairs={{1,0},{2,1},{3,2},{4,3},{5,4},{6,5},{7,6},{8,7},{9,8},{10,9},{11,1... | collective-permute-start | bytes 3145736 | tf_op jit(solution)/shard_map/ppermute | solution.py:13
  53.0 166.9 %copy-start.2 = (f32[256]{0:T(256)S(1)}, f32[256]{0:T(256)}, u32[]{:S(2)}) copy-start(f32[256]{0:T(256)} %param.12) | copy-start | bytes 3076
  53.1 229.9 %copy-start.1 = (f32[256]{0:T(256)S(1)}, f32[256]{0:T(256)}, u32[]{:S(2)}) copy-start(f32[256]{0:T(256)} %param.13) | copy-start | bytes 3076
  66.6 365.2 %reduce-scatter.2.cloned.1.call-start = ((), (), s32[]{:S(2)}) async-start(), calls=%async_computation.1 | async-start | bytes 1462272 | tf_op jit(solution)/shard_map/reduce_scatter | solution.py:104
  284.1 20.8 %collective-permute-start.1 = (f32[256,256]{1,0:T(8,128)}, f32[256,256]{1,0:T(8,128)S(1)}, u32[]{:S(2)}, u32[]{:S(2)}) collective-permute-start(f32[256,256]{1,0:T(8,128)} %get-tuple-element.171), channel_id=1, source_target_pairs={{0,1},{1,2},{2,3},{3,4},{4,5},{5,6},{6,7},{7,8},{8,9},{9,10},{10,1... | collective-permute-start | bytes 786440 | tf_op jit(solution)/shard_map/ppermute | solution.py:13
  298.1 5.6 %collective-permute-start.3 = (f32[1,256]{1,0:T(1,128)S(1)}, f32[1,256]{1,0:T(1,128)S(1)}, u32[]{:S(2)}, u32[]{:S(2)}) collective-permute-start(f32[1,256]{1,0:T(1,128)S(1)} %fusion.75), channel_id=1, source_target_pairs={{1,0},{2,1},{3,2},{4,3},{5,4},{6,5},{7,6},{8,7},{9,8},{10,9},{11,1... | collective-permute-start | bytes 3080 | tf_op jit(solution)/shard_map/ppermute | solution.py:24
  300.0 4.9 %collective-permute-start.2 = (f32[1,256]{1,0:T(1,128)S(1)}, f32[1,256]{1,0:T(1,128)S(1)}, u32[]{:S(2)}, u32[]{:S(2)}) collective-permute-start(f32[1,256]{1,0:T(1,128)S(1)} %fusion.75), channel_id=1, source_target_pairs={{0,1},{1,2},{2,3},{3,4},{4,5},{5,6},{6,7},{7,8},{8,9},{9,10},{10,1... | collective-permute-start | bytes 3080 | tf_op jit(solution)/shard_map/ppermute | solution.py:21
  306.4 5.6 %collective-permute-start.5 = (f32[1,256]{1,0:T(1,128)S(1)}, f32[1,256]{1,0:T(1,128)S(1)}, u32[]{:S(2)}, u32[]{:S(2)}) collective-permute-start(f32[1,256]{1,0:T(1,128)S(1)} %broadcast_select_fusion.2), channel_id=1, source_target_pairs={{1,0},{2,1},{3,2},{4,3},{5,4},{6,5},{7,6},{8,7},{9,8},{10,9},{11,1... | collective-permute-start | bytes 3080 | tf_op jit(solution)/shard_map/ppermute | solution.py:24
  308.3 4.9 %collective-permute-start.4 = (f32[1,256]{1,0:T(1,128)S(1)}, f32[1,256]{1,0:T(1,128)S(1)}, u32[]{:S(2)}, u32[]{:S(2)}) collective-permute-start(f32[1,256]{1,0:T(1,128)S(1)} %broadcast_select_fusion.2), channel_id=1, source_target_pairs={{0,1},{1,2},{2,3},{3,4},{4,5},{5,6},{6,7},{7,8},{8,9},{9,10},{10,1... | collective-permute-start | bytes 3080 | tf_op jit(solution)/shard_map/ppermute | solution.py:21
  314.7 5.6 %collective-permute-start.7 = (f32[1,256]{1,0:T(1,128)S(1)}, f32[1,256]{1,0:T(1,128)S(1)}, u32[]{:S(2)}, u32[]{:S(2)}) collective-permute-start(f32[1,256]{1,0:T(1,128)S(1)} %broadcast_select_fusion.3), channel_id=1, source_target_pairs={{1,0},{2,1},{3,2},{4,3},{5,4},{6,5},{7,6},{8,7},{9,8},{10,9},{11,1... | collective-permute-start | bytes 3080 | tf_op jit(solution)/shard_map/ppermute | solution.py:24
  316.7 4.9 %collective-permute-start.6 = (f32[1,256]{1,0:T(1,128)S(1)}, f32[1,256]{1,0:T(1,128)S(1)}, u32[]{:S(2)}, u32[]{:S(2)}) collective-permute-start(f32[1,256]{1,0:T(1,128)S(1)} %broadcast_select_fusion.3), channel_id=1, source_target_pairs={{0,1},{1,2},{2,3},{3,4},{4,5},{5,6},{6,7},{7,8},{8,9},{9,10},{10,1... | collective-permute-start | bytes 3080 | tf_op jit(solution)/shard_map/ppermute | solution.py:21
  323.1 110.2 %copy-start.3 = (f32[256,1]{0,1:T(1,128)}, f32[256,1]{0,1:T(1,128)S(1)}, u32[]{:S(2)}) copy-start(f32[256,1]{0,1:T(1,128)S(1)} %broadcast_select_fusion.4) | copy-start | bytes 3076
Sparse Core Ops, SparseCore 0:
  66.7 153.1 all-reduce.3
  332.9 98.7 reduce-scatter.1
where the time goes:
time: 449 us; the launch traced here: 441 us
  waiting for transfers between devices  252 us (56%)
  other arithmetic  71.2 us (16%)
  matrix products  57.2 us (13%)
  starting transfers between devices  36.2 us (8%)
  between operations  16.4 us (4%)
  local copies, waits for them, and re-layouts  7.24 us (2%)
    psum x1, waiting for transfers between devices, shards(): diag_sum, upper_sum = lax.psum((diag_part, upper_part), 'scen')  153 us
    reduce_scatter x1, waiting for transfers between devices, shards(): lax.psum_scatter(partial_terms, 'link', scatter_dimension=1, tiled=True)  98.9 us
    another operation x7, other arithmetic, shards(): factor = jnp.linalg.cholesky(schur_diag)  34.6 us
    another operation x4, other arithmetic, chol_apply(): lax.linalg.triangular_solve(factor, inner, left_side=True, lower=True, tr...  19.7 us
    ppermute x2, starting transfers between devices, shifted(): return lax.ppermute(shard, axis, pairs)  19.2 us
    dot_general x2, matrix products, contract_slots(): lax.dot_general(left, right, (((0, 1), (0, 1)), ((), ())), preferred_elem...  13.6 us
    dot_general x1, matrix products, shards(): jnp.einsum('jc,cnr->jnr', up_low.astype(jnp.bfloat16), scaled, preferred_...  12.2 us
    dot_general x1, matrix products, shards(): jnp.einsum('jc,cnr->jnr', down_high.astype(jnp.bfloat16), link_rows, pref...  12.2 us
  transfers between devices with their start and end apart: 10, of which 2 were waited for; matrix products, arithmetic and copies ran while one was open for 10% of the time, Pallas kernels for 0%

commit v1 on v0

v1 whole, which is shorter than its diff:
```python
import functools

import jax
import jax.numpy as jnp
from jax import lax
from jax.experimental import pallas as pl
from jax.experimental.pallas import tpu as pltpu
from jax.sharding import PartitionSpec as P

SWEEPS = 2
HALF = 128
TILE = 256
PANEL = 32
HIGHEST = lax.Precision.HIGHEST
MESH = pl.DeviceIdType.MESH
BF16 = jnp.bfloat16
F32 = jnp.float32


def dot_tt(left, right):
    return lax.dot_general(
        left, right, (((0,), (0,)), ((), ())), precision=HIGHEST, preferred_element_type=F32
    )


def tree_sum(terms):
    while len(terms) > 1:
        pairs = [terms[i] + terms[i + 1] for i in range(0, len(terms) - 1, 2)]
        terms = pairs + terms[len(terms) - len(terms) % 2 :]
    return terms[0]


def pair_sweep(held, count, first):
    second = first + 1

    def get(i, j):
        return held[(min(i, j), max(i, j))]

    a, b, c = get(first, first), get(first, second), get(second, second)
    scale = 1.0 / (a * c - b * b)
    inv_a, inv_b, inv_c = c * scale, -(b * scale), a * scale
    others = [i for i in range(count) if i not in (first, second)]
    row0 = {i: inv_a * get(first, i) + inv_b * get(second, i) for i in others}
    row1 = {i: inv_b * get(first, i) + inv_c * get(second, i) for i in others}
    new = {}
    for at, i in enumerate(others):
        for j in others[at:]:
            new[(i, j)] = get(i, j) - (get(first, i) * row0[j] + get(second, i) * row1[j])
        new[(min(i, first), max(i, first))] = row0[i]
        new[(min(i, second), max(i, second))] = row1[i]
    new[(first, first)] = -inv_a
    new[(first, second)] = -inv_b
    new[(second, second)] = -inv_c
    return new


def panel_sweep(panel, start):
    rows, width = panel.shape
    lane = lax.broadcasted_iota(jnp.int32, (1, width), 1)
    sub = lax.broadcasted_iota(jnp.int32, (8, 1), 0)

    def wide(v):
        return jnp.concatenate([v] * (width // HALF), axis=1)

    for top in range(0, rows, 8):
        at = start + top
        own = panel[top : top + 8, :]
        columns = [panel[:, at + j : at + j + 1] for j in range(8)]
        held = {}
        for j in range(8):
            spread = jnp.broadcast_to(columns[j][top : top + 8], (8, HALF))
            for i in range(j + 1):
                held[(i, j)] = jnp.broadcast_to(spread[i : i + 1], (8, HALF))
        for first in range(0, 8, 2):
            held = pair_sweep(held, 8, first)
        inverse = []
        for j in range(8):
            column = held[(0, j)]
            for i in range(1, 8):
                column = jnp.where(sub == i, held[(min(i, j), max(i, j))], column)
            inverse.append(column)
        swept = -tree_sum([wide(inverse[j]) * own[j : j + 1, :] for j in range(8)])
        for j in range(8):
            swept = jnp.where(lane == at + j, wide(inverse[j]), swept)
        inside = (lane >= at) & (lane < at + 8)
        rest = jnp.where(inside, 0.0, panel) - tree_sum(
            [columns[j] * swept[j : j + 1, :] for j in range(8)]
        )
        parts = [rest[:top]] if top else []
        parts.append(swept)
        if top + 8 < rows:
            parts.append(rest[top + 8 :])
        panel = jnp.concatenate(parts, axis=0)
    return panel


def sweep_rows(matrix, start):
    before = matrix[start : start + PANEL, :]
    after = panel_sweep(before, start)
    lane = lax.broadcasted_iota(jnp.int32, (1, TILE), 1)
    inside = (lane >= start) & (lane < start + PANEL)
    matrix[...] = jnp.where(inside, 0.0, matrix[...]) - dot_tt(before, after)
    matrix[start : start + PANEL, :] = after


def kernel(
    scens,
    links,
    ids_s,
    ids_v,
    rows_hbm,
    scaling_hbm,
    regulariser,
    right_side,
    direction_out,
    step_out,
    rows,
    scaling,
    total,
    part,
    gathered,
    full,
    matrix,
    down_rows,
    next_rows,
    upper_part,
    upper_gathered,
    upper_full,
    current,
    vec_send,
    vec_recv,
    spread,
    slot_send,
    slot_recv,
    row_sems,
    scaling_sem,
    part_send,
    part_recv,
    full_send,
    full_recv,
    next_send,
    next_recv,
    upart_send,
    upart_recv,
    ufull_send,
    ufull_recv,
    vsend_sems,
    vrecv_sems,
    slot_send_sems,
    slot_recv_sems,
):
    me_s = lax.axis_index("scen")
    me_t = lax.axis_index("link")
    slots, width, _ = rows.shape
    scen_count = scaling.shape[0]
    pieces = width // links
    chunk = part.shape[0] // scens
    uchunk = upper_part.shape[0] // scens

    def scen_peer(k):
        return lax.rem(me_s + k, scens)

    def scen_source(k):
        return lax.rem(me_s + scens - k, scens)

    def link_peer(k):
        return lax.rem(me_t + k, links)

    def link_source(k):
        return lax.rem(me_t + links - k, links)

    vec_recv[...] = jnp.zeros_like(vec_recv)
    barrier = pltpu.get_barrier_semaphore()
    for k in range(1, scens):
        pl.semaphore_signal(barrier, 1, device_id={"scen": scen_peer(k)}, device_id_type=MESH)
    for k in range(1, links):
        pl.semaphore_signal(barrier, 1, device_id={"link": link_peer(k)}, device_id_type=MESH)

    scaling_copy = pltpu.make_async_copy(scaling_hbm, scaling, scaling_sem)
    scaling_copy.start()
    for c in range(slots):
        pltpu.make_async_copy(rows_hbm.at[c], rows.at[c], row_sems.at[c]).start()

    next_t = jnp.minimum(me_t + 1, links - 1)
    prev_t = jnp.maximum(me_t - 1, 0)
    here = [ids_s[c, me_t] for c in range(slots)]
    after = [ids_s[c, next_t] for c in range(slots)]
    before = [ids_s[c, prev_t] for c in range(slots)]
    up_slot, up_found, down_slot = jnp.int32(0), jnp.int32(0), jnp.int32(0)
    for c in range(slots):
        up_hit, down_hit = jnp.int32(0), jnp.int32(0)
        for other in range(slots):
            up_hit = up_hit | (here[c] == after[other]).astype(jnp.int32)
            down_hit = down_hit | (here[c] == before[other]).astype(jnp.int32)
        live = (here[c] < scen_count).astype(jnp.int32)
        up_hit = up_hit * live
        down_hit = down_hit * live
        up_slot = jnp.where(up_hit > 0, c, up_slot)
        up_found = up_found | up_hit
        down_slot = jnp.where(down_hit > 0, c, down_slot)
    up_found = jnp.where(me_t + 1 < links, up_found, 0)

    spread[...] = jnp.zeros_like(spread)
    names = lax.broadcasted_iota(jnp.int32, (slots, TILE), 1)
    for t in range(links):
        spread[t * 16 : t * 16 + slots, :] = (ids_v[:, t : t + 1] == names).astype(F32)
    slot_send[...] = jnp.zeros_like(slot_send)

    def scale_row(name, keep):
        row = scaling[pl.ds(jnp.minimum(name, scen_count - 1), 1), :]
        return row * keep.astype(F32)

    total[...] = jnp.zeros_like(total)
    scaling_copy.wait()

    @pl.loop(0, slots)
    def _(c):
        pltpu.make_async_copy(rows_hbm.at[c], rows.at[c], row_sems.at[c]).wait()
        name = ids_s[c, me_t]
        row = scale_row(name, (name < scen_count).astype(jnp.int32))
        terms = []
        for at in range(0, width, TILE):
            block = rows[c, at : at + TILE, :]
            scaled = (block.T.astype(F32) * row[:, at : at + TILE]).astype(BF16)
            terms.append(jnp.dot(scaled, block, preferred_element_type=F32))
        summed = terms[0]
        for term in terms[1:]:
            summed = summed + term
        total[...] += summed

    low, high = total[:HALF, :HALF], total[HALF:, HALF:]
    part[:HALF, :] = 0.5 * (low + low.T)
    part[HALF : 2 * HALF, :] = 0.5 * (total[HALF:, :HALF] + total[:HALF, HALF:].T)
    part[2 * HALF :, :] = 0.5 * (high + high.T)

    pl.semaphore_wait(barrier, scens + links - 2)

    def part_copy(k):
        peer = scen_peer(k)
        return pltpu.make_async_remote_copy(
            src_ref=part.at[pl.ds(pl.multiple_of(peer * chunk, 8), chunk)],
            dst_ref=gathered.at[me_s],
            send_sem=part_send.at[k],
            recv_sem=part_recv.at[me_s],
            device_id={"scen": peer},
            device_id_type=MESH,
        )

    def part_wait(k):
        source = scen_source(k)
        pltpu.make_async_remote_copy(
            src_ref=part.at[pl.ds(0, chunk)],
            dst_ref=gathered.at[source],
            send_sem=part_send.at[k],
            recv_sem=part_recv.at[source],
            device_id={"scen": source},
            device_id_type=MESH,
        ).wait_recv()

    def full_copy(k):
        mine = pl.ds(pl.multiple_of(me_s * chunk, 8), chunk)
        return pltpu.make_async_remote_copy(
            src_ref=full.at[mine],
            dst_ref=full.at[mine],
            send_sem=full_send.at[k],
            recv_sem=full_recv.at[me_s],
            device_id={"scen": scen_peer(k)},
            device_id_type=MESH,
        )

    def full_wait(k):
        source = scen_source(k)
        theirs = pl.ds(pl.multiple_of(source * chunk, 8), chunk)
        pltpu.make_async_remote_copy(
            src_ref=full.at[theirs],
            dst_ref=full.at[theirs],
            send_sem=full_send.at[k],
            recv_sem=full_recv.at[source],
            device_id={"scen": source},
            device_id_type=MESH,
        ).wait_recv()

    def upart_copy(k):
        peer = scen_peer(k)
        return pltpu.make_async_remote_copy(
            src_ref=upper_part.at[pl.ds(pl.multiple_of(peer * uchunk, 16), uchunk)],
            dst_ref=upper_gathered.at[me_s],
            send_sem=upart_send.at[k],
            recv_sem=upart_recv.at[me_s],
            device_id={"scen": peer},
            device_id_type=MESH,
        )

    def upart_wait(k):
        source = scen_source(k)
        pltpu.make_async_remote_copy(
            src_ref=upper_part.at[pl.ds(0, uchunk)],
            dst_ref=upper_gathered.at[source],
            send_sem=upart_send.at[k],
            recv_sem=upart_recv.at[source],
            device_id={"scen": source},
            device_id_type=MESH,
        ).wait_recv()

    def ufull_copy(k):
        mine = pl.ds(pl.multiple_of(me_s * uchunk, 16), uchunk)
        return pltpu.make_async_remote_copy(
            src_ref=upper_full.at[mine],
            dst_ref=upper_full.at[mine],
            send_sem=ufull_send.at[k],
            recv_sem=ufull_recv.at[me_s],
            device_id={"scen": scen_peer(k)},
            device_id_type=MESH,
        )

    def ufull_wait(k):
        source = scen_source(k)
        theirs = pl.ds(pl.multiple_of(source * uchunk, 16), uchunk)
        pltpu.make_async_remote_copy(
            src_ref=upper_full.at[theirs],
            dst_ref=upper_full.at[theirs],
            send_sem=ufull_send.at[k],
            recv_sem=ufull_recv.at[source],
            device_id={"scen": source},
            device_id_type=MESH,
        ).wait_recv()

    @pl.loop(1, scens)
    def _(k):
        part_copy(k).start()

    @pl.loop(0, width // TILE)
    def _(j):
        at = pl.ds(pl.multiple_of(j * TILE, TILE), TILE)
        down_rows[at, :] = rows[down_slot, at, :]

    next_copy = pltpu.make_async_remote_copy(
        src_ref=down_rows,
        dst_ref=next_rows,
        send_sem=next_send,
        recv_sem=next_recv,
        device_id={"link": link_source(1)},
        device_id_type=MESH,
    )

    @pl.when(me_t > 0)
    def _():
        next_copy.start()

    gathered[me_s] = part[pl.ds(pl.multiple_of(me_s * chunk, 8), chunk), :]

    @pl.loop(1, scens)
    def _(k):
        part_wait(k)

    full[pl.ds(pl.multiple_of(me_s * chunk, 8), chunk), :] = tree_sum(
        [gathered[i] for i in range(scens)]
    )

    @pl.loop(1, scens)
    def _(k):
        full_copy(k).start()

    @pl.loop(1, scens)
    def _(k):
        full_wait(k)

    corner = full[HALF : 2 * HALF, :]
    matrix[:HALF, :HALF] = full[:HALF, :]
    matrix[HALF:, :HALF] = corner
    matrix[:HALF, HALF:] = corner.T
    matrix[HALF:, HALF:] = full[2 * HALF :, :]
    on_diag = lax.broadcasted_iota(jnp.int32, (TILE, TILE), 0) == lax.broadcasted_iota(
        jnp.int32, (TILE, TILE), 1
    )
    matrix[...] += jnp.where(on_diag, regulariser[...], 0.0)

    def upper_terms():
        @pl.when(me_t + 1 < links)
        def _():
            next_copy.wait_recv()

        @pl.when(me_t + 1 == links)
        def _():
            next_rows[...] = jnp.zeros_like(next_rows)

        row = scale_row(ids_s[up_slot, me_t], up_found)
        terms = []
        for at in range(0, width, TILE):
            block = rows[up_slot, at : at + TILE, :]
            scaled = (block.T.astype(F32) * row[:, at : at + TILE]).astype(BF16)
            terms.append(
                jnp.dot(scaled, next_rows[at : at + TILE, :], preferred_element_type=F32)
            )
        summed = tree_sum(terms).astype(BF16)
        upper_part[:TILE, :] = summed[:, :HALF]
        upper_part[TILE:, :] = summed[:, HALF:]

        @pl.loop(1, scens)
        def _(k):
            upart_copy(k).start()

        upper_gathered[me_s] = upper_part[pl.ds(pl.multiple_of(me_s * uchunk, 16), uchunk), :]

    def upper_sum():
        @pl.loop(1, scens)
        def _(k):
            upart_wait(k)

        upper_full[pl.ds(pl.multiple_of(me_s * uchunk, 16), uchunk), :] = tree_sum(
            [upper_gathered[i].astype(F32) for i in range(scens)]
        ).astype(BF16)

        @pl.loop(1, scens)
        def _(k):
            ufull_copy(k).start()

    for at in range(0, TILE, PANEL):
        sweep_rows(matrix, at)
        if at == 3 * PANEL:
            upper_terms()
        if at == 6 * PANEL:
            upper_sum()

    def solve(vector):
        wide = jnp.broadcast_to(vector, (8, TILE))
        found = -jnp.dot(wide, matrix[...], precision=HIGHEST, preferred_element_type=F32)
        return found[:1, :]

    def split(vector):
        first = vector.astype(BF16)
        left = vector - first.astype(F32)
        second = left.astype(BF16)
        third = (left - second.astype(F32)).astype(BF16)
        parts = [jnp.broadcast_to(v.astype(F32), (8, TILE)) for v in (first, second, third)]
        sub = lax.broadcasted_iota(jnp.int32, (8, TILE), 0)
        mixed = jnp.where(sub == 0, parts[0], jnp.where(sub == 1, parts[1], parts[2]))
        return jnp.where(sub < 3, mixed, 0.0).astype(BF16)

    def to_next(vector):
        parts = split(vector)
        low = jnp.dot(parts, upper_full[:TILE, :], preferred_element_type=F32)
        high = jnp.dot(parts, upper_full[TILE:, :], preferred_element_type=F32)
        return jnp.sum(jnp.concatenate([low, high], axis=1), axis=0, keepdims=True)

    def from_next(vector):
        parts = split(vector)
        turned = (((1,), (1,)), ((), ()))
        low = lax.dot_general(
            parts[:, :HALF], upper_full[:TILE, :], turned, preferred_element_type=F32
        )
        high = lax.dot_general(
            parts[:, HALF:], upper_full[TILE:, :], turned, preferred_element_type=F32
        )
        return jnp.sum(low + high, axis=0, keepdims=True)

    def put(ref, vector):
        ref[0:1, :] = vector[:, :HALF]
        ref[1:2, :] = vector[:, HALF:]

    def fetch(ref):
        return jnp.concatenate([ref[0:1, :], ref[1:2, :]], axis=1)

    def vec_copy(step, side):
        return pltpu.make_async_remote_copy(
            src_ref=vec_send.at[2 * step + side],
            dst_ref=vec_recv.at[2 * step + side],
            send_sem=vsend_sems.at[2 * step + side],
            recv_sem=vrecv_sems.at[2 * step + side],
            device_id={"link": link_source(1) if side == 0 else link_peer(1)},
            device_id_type=MESH,
        )

    colour = lax.rem(me_t, 2)
    vec_send[...] = jnp.zeros_like(vec_send)
    current[...] = jnp.zeros_like(current)

    @pl.when(colour == 0)
    def _():
        current[...] = solve(right_side[...])

    @pl.loop(1, scens)
    def _(k):
        ufull_wait(k)

    for step in range(2 * SWEEPS - 1):

        @pl.when(colour == step % 2)
        def _():
            @pl.when(me_t > 0)
            def _():
                put(vec_send.at[2 * step], current[...])
                vec_copy(step, 0).start()

            @pl.when(me_t + 1 < links)
            def _():
                put(vec_send.at[2 * step + 1], to_next(current[...]))
                vec_copy(step, 1).start()

        @pl.when(colour != step % 2)
        def _():
            @pl.when(me_t + 1 < links)
            def _():
                vec_copy(step, 0).wait_recv()

            coupled = from_next(fetch(vec_recv.at[2 * step]))

            @pl.when(me_t > 0)
            def _():
                vec_copy(step, 1).wait_recv()

            coupled = coupled + fetch(vec_recv.at[2 * step + 1])
            current[...] = solve(right_side[...] - coupled)

    direction_out[...] = current[...]

    half = jnp.broadcast_to(current[...].astype(BF16), (16, TILE))

    @pl.loop(0, slots)
    def _(c):
        for j in range(links):
            value = lax.dot_general(
                half,
                rows[c, j * pieces : (j + 1) * pieces, :],
                (((1,), (1,)), ((), ())),
                preferred_element_type=F32,
            )
            slot_send[j, pl.ds(c, 1), :] = value[:1, :]

    def slot_copy(k):
        peer = link_peer(k)
        return pltpu.make_async_remote_copy(
            src_ref=slot_send.at[peer],
            dst_ref=slot_recv.at[me_t],
            send_sem=slot_send_sems.at[k],
            recv_sem=slot_recv_sems.at[me_t],
            device_id={"link": peer},
            device_id_type=MESH,
        )

    @pl.loop(1, links)
    def _(k):
        slot_copy(k).start()

    slot_recv[me_t] = slot_send[me_t]

    @pl.loop(1, links)
    def _(k):
        source = link_source(k)
        pltpu.make_async_remote_copy(
            src_ref=slot_send.at[source],
            dst_ref=slot_recv.at[source],
            send_sem=slot_send_sems.at[k],
            recv_sem=slot_recv_sems.at[source],
            device_id={"link": source},
            device_id_type=MESH,
        ).wait_recv()

    values = slot_recv[...].reshape(links * 16, pieces)
    summed = dot_tt(spread[...], values)
    columns = scaling[:, pl.ds(pl.multiple_of(me_t * pieces, HALF), pieces)]
    step_out[...] = columns * summed[:scen_count, :]

    @pl.loop(1, scens)
    def _(k):
        part_copy(k).wait_send()
        full_copy(k).wait_send()
        upart_copy(k).wait_send()
        ufull_copy(k).wait_send()

    @pl.when(me_t > 0)
    def _():
        next_copy.wait_send()

    for step in range(2 * SWEEPS - 1):

        @pl.when(colour == step % 2)
        def _():
            @pl.when(me_t > 0)
            def _():
                vec_copy(step, 0).wait_send()

            @pl.when(me_t + 1 < links)
            def _():
                vec_copy(step, 1).wait_send()

    @pl.loop(1, links)
    def _(k):
        slot_copy(k).wait_send()


def shards(link_rows, slot_scenario, diag_scaling, regulariser, right_side):
    scens, links = lax.axis_size("scen"), lax.axis_size("link")
    slots, width, _ = link_rows.shape
    scen_count = diag_scaling.shape[0]
    pieces = width // links
    steps = 2 * SWEEPS - 1
    vmem = pl.BlockSpec(memory_space=pltpu.VMEM)
    dma = pltpu.SemaphoreType.DMA
    direction, step = pl.pallas_call(
        functools.partial(kernel, scens, links),
        out_shape=(
            jax.ShapeDtypeStruct((1, TILE), F32),
            jax.ShapeDtypeStruct((scen_count, pieces), F32),
        ),
        in_specs=[
            pl.BlockSpec(memory_space=pltpu.SMEM),
            vmem,
            pl.BlockSpec(memory_space=pl.ANY),
            pl.BlockSpec(memory_space=pl.ANY),
            vmem,
            vmem,
        ],
        out_specs=(vmem, vmem),
        scratch_shapes=[
            pltpu.VMEM((slots, width, TILE), BF16),
            pltpu.VMEM((scen_count, width), F32),
            pltpu.VMEM((TILE, TILE), F32),
            pltpu.VMEM((3 * HALF, HALF), F32),
            pltpu.VMEM((scens, 3 * HALF // scens, HALF), F32),
            pltpu.VMEM((3 * HALF, HALF), F32),
            pltpu.VMEM((TILE, TILE), F32),
            pltpu.VMEM((width, TILE), BF16),
            pltpu.VMEM((width, TILE), BF16),
            pltpu.VMEM((2 * TILE, HALF), BF16),
            pltpu.VMEM((scens, 2 * TILE // scens, HALF), BF16),
            pltpu.VMEM((2 * TILE, HALF), BF16),
            pltpu.VMEM((1, TILE), F32),
            pltpu.VMEM((2 * steps, 8, HALF), F32),
            pltpu.VMEM((2 * steps, 8, HALF), F32),
            pltpu.VMEM((links * 16, TILE), F32),
            pltpu.VMEM((links, 16, pieces), F32),
            pltpu.VMEM((links, 16, pieces), F32),
            dma((slots,)),
            dma,
            dma((scens,)),
            dma((scens,)),
            dma((scens,)),
            dma((scens,)),
            dma,
            dma,
            dma((scens,)),
            dma((scens,)),
            dma((scens,)),
            dma((scens,)),
            dma((2 * steps,)),
            dma((2 * steps,)),
            dma((links,)),
            dma((links,)),
        ],
        compiler_params=pltpu.CompilerParams(
            collective_id=0, has_side_effects=True, vmem_limit_bytes=56 * 2**20
        ),
        name="coloured_sweeps",
    )(
        slot_scenario,
        slot_scenario,
        link_rows,
        diag_scaling,
        regulariser.reshape(1, TILE),
        right_side.reshape(1, TILE),
    )
    return direction.reshape(TILE), step


def solution(mesh):
    in_specs = (P("scen", None, "link"), P("scen", None), P("scen", None), P("link"), P("link"))
    out_specs = (P("link"), P("scen", "link"))
    return jax.shard_map(shards, mesh=mesh, in_specs=in_specs, out_specs=out_specs, check_vma=False)
```

time: 449 us -> 100 us (0.22); the launches traced: 441 us -> 99.8 us
  waiting for transfers between devices: 252 us -> 0 us
  Pallas kernels: 0 us -> 96.4 us
  other arithmetic: 71.2 us -> 0 us
  matrix products: 57.2 us -> 0 us
  starting transfers between devices: 36.2 us -> 0 us
  between operations: 16.4 us -> 0.64 us
    psum x1 -> x0, waiting for transfers between devices: 153 us -> none  [shards(): diag_sum, upper_sum = lax.psum((diag_part, upper_part), 'scen')]
    reduce_scatter x1 -> x0, waiting for transfers between devices: 98.9 us -> none  [shards(): lax.psum_scatter(partial_terms, 'link', scatter_dimension=1, tiled=True)]
    pallas_call x0 -> x1, Pallas kernels: none -> 96.4 us  [shards(): pl.pallas_call(functools.partial(kernel, scens, links), out_shape=(jax.Sh...]
    another operation x13 -> x0, other arithmetic: 54.7 us -> none  [the longest x7 34.6 us: shards(): factor = jnp.linalg.cholesky(schur_diag)]
    dot_general x13 -> x0, matrix products: 52.2 us -> none  [the longest x2 13.6 us: contract_slots(): lax.dot_general(left, right, (((0, 1), (0, 1)), ((), ())), preferred_elem...]
    ppermute x8 -> x0, starting transfers between devices: 35.9 us -> none  [the longest x2 19.2 us: shifted(): return lax.ppermute(shard, axis, pairs)]
    convert_element_type x3 -> x0, other arithmetic: 11.7 us -> none  [the longest x1 11.6 us: shards(): scaled = (link_rows * slot_scale[:, :, None]).astype(jnp.bfloat16)]
    another operation x26 -> x0, matrix products: 5.05 us -> none  [the longest x12 2.56 us: chol_apply(): lax.linalg.triangular_solve(factor, inner, left_side=True, lower=True, tr...]
  transfers between devices with their start and end apart: 10 -> 0, of which waited for: 2 -> 0; matrix products, arithmetic and copies ran while one was open for 10% -> 0% of each run, Pallas kernels for 0% -> 0%
where the time goes in v1:
time: 100 us; the launch traced here: 99.8 us
  Pallas kernels  96.4 us (96%)
  local copies, waits for them, and re-layouts  2.77 us (3%)
    pallas_call x1, Pallas kernels, shards(): pl.pallas_call(functools.partial(kernel, scens, links), out_shape=(jax.Sh...  96.4 us
    unnamed x2, local copies, waits for them, and re-layouts  2.77 us

profile of v1, /device:TPU:1, one launch (start us, length us, event | category | flops | bytes accessed | tf_op | source)
XLA Modules:
  0.0 99.8 jit_solution(12630077073017452426)
XLA Ops:
  0.6 96.4 %coloured_sweeps.1 = (f32[1,256]{1,0:T(1,128)}, f32[162,128]{1,0:T(8,128)}) custom-call(s32[12,16]{1,0:T(8,128)} %ids_v.1, s32[12,16]{1,0:T(8,128)} %ids_v.1, bf16[12,2048,256]{2,1,0:T(8,128)(2,1)} %rows_hbm.1, f32[162,2048]{1,0:T(8,128)} %scaling_hbm.1, f32[1,256]{1,0:T(1,128)} %bitcast.3, f32[1,256]{1,0:T(1,128)} %bitcast.4), custom_call_target="tpu_custom_call" | custom-call | tf_op jit(solution)/shard_map/coloured_sweeps/pallas_call | solution.py:600
  97.1 1.2 %copy.9 = f32[256]{0:T(256)} copy(f32[256]{0:T(256)} %bitcast.5) | data formatting | bytes 2048
  98.3 1.5 %copy.10 = f32[162,128]{1,0:T(8,128)} copy(f32[162,128]{1,0:T(8,128)} %get-tuple-element.9) | data formatting | bytes 165888

commit v2 on v1

--- a/solution.py
+++ b/solution.py
@@ -121,9 +121,13 @@
     gathered,
     full,
     matrix,
-    down_rows,
-    next_rows,
+    up_keep,
+    up_send,
+    up_got,
+    down_send,
+    down_got,
     upper_part,
+    below_part,
     upper_gathered,
     upper_full,
     current,
@@ -138,10 +142,12 @@
     part_recv,
     full_send,
     full_recv,
-    next_send,
-    next_recv,
+    up_sems,
+    down_sems,
     upart_send,
     upart_recv,
+    bpart_send,
+    bpart_recv,
     ufull_send,
     ufull_recv,
     vsend_sems,
@@ -169,17 +175,28 @@
     def link_source(k):
         return lax.rem(me_t + links - k, links)
 
-    vec_recv[...] = jnp.zeros_like(vec_recv)
-    barrier = pltpu.get_barrier_semaphore()
-    for k in range(1, scens):
-        pl.semaphore_signal(barrier, 1, device_id={"scen": scen_peer(k)}, device_id_type=MESH)
-    for k in range(1, links):
-        pl.semaphore_signal(barrier, 1, device_id={"link": link_peer(k)}, device_id_type=MESH)
-
     scaling_copy = pltpu.make_async_copy(scaling_hbm, scaling, scaling_sem)
     scaling_copy.start()
     for c in range(slots):
         pltpu.make_async_copy(rows_hbm.at[c], rows.at[c], row_sems.at[c]).start()
+
+    vec_recv[...] = jnp.zeros_like(vec_recv)
+    barrier = pltpu.get_barrier_semaphore()
+
+    def greet(scen, link):
+        pl.semaphore_signal(
+            barrier, 1, device_id={"scen": scen, "link": link}, device_id_type=MESH
+        )
+
+    @pl.loop(1, scens)
+    def _(k):
+        greet(scen_peer(k), me_t)
+        greet(scen_peer(k), link_peer(1))
+        greet(scen_peer(k), link_source(1))
+
+    @pl.loop(1, links)
+    def _(k):
+        greet(me_s, link_peer(k))
 
     next_t = jnp.minimum(me_t + 1, links - 1)
     prev_t = jnp.maximum(me_t - 1, 0)
@@ -213,9 +230,7 @@
     total[...] = jnp.zeros_like(total)
     scaling_copy.wait()
 
-    @pl.loop(0, slots)
-    def _(c):
-        pltpu.make_async_copy(rows_hbm.at[c], rows.at[c], row_sems.at[c]).wait()
+    def add_slot(c):
         name = ids_s[c, me_t]
         row = scale_row(name, (name < scen_count).astype(jnp.int32))
         terms = []
@@ -228,12 +243,72 @@
             summed = summed + term
         total[...] += summed
 
+    def arrived(c):
+        pltpu.make_async_copy(rows_hbm.at[c], rows.at[c], row_sems.at[c]).wait()
+
+    early = slots // 2
+
+    @pl.loop(0, early)
+    def _(c):
+        arrived(c)
+        add_slot(c)
+
+    @pl.loop(early, slots)
+    def _(c):
+        arrived(c)
+
+    part_width = width // 2
+    up_row = scale_row(ids_s[up_slot, me_t], up_found)
+    for at in range(0, part_width, TILE):
+        down_send[at : at + TILE, :] = rows[down_slot, at : at + TILE, :]
+    for at in range(0, part_width, TILE):
+        beyond = part_width + at
+        block = rows[up_slot, beyond : beyond + TILE, :]
+        up_send[:, at : at + TILE] = (
+            block.T.astype(F32) * up_row[:, beyond : beyond + TILE]
+        ).astype(BF16)
+
+    pl.semaphore_wait(barrier, 3 * (scens - 1) + links - 1)
+
+    down_copy = pltpu.make_async_remote_copy(
+        src_ref=down_send,
+        dst_ref=down_got,
+        send_sem=down_sems.at[0],
+        recv_sem=down_sems.at[1],
+        device_id={"link": link_source(1)},
+        device_id_type=MESH,
+    )
+    up_copy = pltpu.make_async_remote_copy(
+        src_ref=up_send,
+        dst_ref=up_got,
+        send_sem=up_sems.at[0],
+        recv_sem=up_sems.at[1],
+        device_id={"link": link_peer(1)},
+        device_id_type=MESH,
+    )
+
+    @pl.when(me_t > 0)
+    def _():
+        down_copy.start()
+
+    @pl.when(me_t + 1 < links)
+    def _():
+        up_copy.start()
+
+    for at in range(0, part_width, TILE):
+        block = rows[up_slot, at : at + TILE, :]
+        up_keep[:, at : at + TILE] = (
+            block.T.astype(F32) * up_row[:, at : at + TILE]
+        ).astype(BF16)
+
+    @pl.loop(early, slots)
+    def _(c):
+        add_slot(c)
+
     low, high = total[:HALF, :HALF], total[HALF:, HALF:]
     part[:HALF, :] = 0.5 * (low + low.T)
     part[HALF : 2 * HALF, :] = 0.5 * (total[HALF:, :HALF] + total[:HALF, HALF:].T)
     part[2 * HALF :, :] = 0.5 * (high + high.T)
-
-    pl.semaphore_wait(barrier, scens + links - 2)
 
     def part_copy(k):
         peer = scen_peer(k)
@@ -302,6 +377,28 @@
             device_id_type=MESH,
         ).wait_recv()
 
+    def bpart_copy(k):
+        peer = scen_peer(k)
+        return pltpu.make_async_remote_copy(
+            src_ref=below_part.at[pl.ds(pl.multiple_of(peer * uchunk, 16), uchunk)],
+            dst_ref=upper_gathered.at[scens + me_s],
+            send_sem=bpart_send.at[k],
+            recv_sem=bpart_recv.at[me_s],
+            device_id={"scen": peer, "link": link_source(1)},
+            device_id_type=MESH,
+        )
+
+    def bpart_wait(k):
+        source = scen_source(k)
+        pltpu.make_async_remote_copy(
+            src_ref=below_part.at[pl.ds(0, uchunk)],
+            dst_ref=upper_gathered.at[scens + source],
+            send_sem=bpart_send.at[k],
+            recv_sem=bpart_recv.at[source],
+            device_id={"scen": source, "link": link_peer(1)},
+            device_id_type=MESH,
+        ).wait_recv()
+
     def ufull_copy(k):
         mine = pl.ds(pl.multiple_of(me_s * uchunk, 16), uchunk)
         return pltpu.make_async_remote_copy(
@@ -329,24 +426,6 @@
     def _(k):
         part_copy(k).start()
 
-    @pl.loop(0, width // TILE)
-    def _(j):
-        at = pl.ds(pl.multiple_of(j * TILE, TILE), TILE)
-        down_rows[at, :] = rows[down_slot, at, :]
-
-    next_copy = pltpu.make_async_remote_copy(
-        src_ref=down_rows,
-        dst_ref=next_rows,
-        send_sem=next_send,
-        recv_sem=next_recv,
-        device_id={"link": link_source(1)},
-        device_id_type=MESH,
-    )
-
-    @pl.when(me_t > 0)
-    def _():
-        next_copy.start()
-
     gathered[me_s] = part[pl.ds(pl.multiple_of(me_s * chunk, 8), chunk), :]
 
     @pl.loop(1, scens)
@@ -375,49 +454,65 @@
     )
     matrix[...] += jnp.where(on_diag, regulariser[...], 0.0)
 
+    def store_wide(ref, value):
+        ref[:TILE, :] = value[:, :HALF].astype(BF16)
+        ref[TILE:, :] = value[:, HALF:].astype(BF16)
+
+    def below_terms():
+        @pl.when(me_t > 0)
+        def _():
+            up_copy.wait_recv()
+            store_wide(
+                below_part,
+                jnp.dot(
+                    up_got[...], rows[down_slot, part_width:, :], preferred_element_type=F32
+                ),
+            )
+
+            @pl.loop(0, scens)
+            def _(k):
+                bpart_copy(k).start()
+
     def upper_terms():
         @pl.when(me_t + 1 < links)
         def _():
-            next_copy.wait_recv()
-
-        @pl.when(me_t + 1 == links)
+            down_copy.wait_recv()
+            store_wide(
+                upper_part,
+                jnp.dot(up_keep[...], down_got[...], preferred_element_type=F32),
+            )
+
+            @pl.loop(1, scens)
+            def _(k):
+                upart_copy(k).start()
+
+            upper_gathered[me_s] = upper_part[
+                pl.ds(pl.multiple_of(me_s * uchunk, 16), uchunk), :
+            ]
+
+    def upper_sum():
+        @pl.when(me_t + 1 < links)
         def _():
-            next_rows[...] = jnp.zeros_like(next_rows)
-
-        row = scale_row(ids_s[up_slot, me_t], up_found)
-        terms = []
-        for at in range(0, width, TILE):
-            block = rows[up_slot, at : at + TILE, :]
-            scaled = (block.T.astype(F32) * row[:, at : at + TILE]).astype(BF16)
-            terms.append(
-                jnp.dot(scaled, next_rows[at : at + TILE, :], preferred_element_type=F32)
-            )
-        summed = tree_sum(terms).astype(BF16)
-        upper_part[:TILE, :] = summed[:, :HALF]
-        upper_part[TILE:, :] = summed[:, HALF:]
-
-        @pl.loop(1, scens)
-        def _(k):
-            upart_copy(k).start()
-
-        upper_gathered[me_s] = upper_part[pl.ds(pl.multiple_of(me_s * uchunk, 16), uchunk), :]
-
-    def upper_sum():
-        @pl.loop(1, scens)
-        def _(k):
-            upart_wait(k)
-
-        upper_full[pl.ds(pl.multiple_of(me_s * uchunk, 16), uchunk), :] = tree_sum(
-            [upper_gathered[i].astype(F32) for i in range(scens)]
-        ).astype(BF16)
-
-        @pl.loop(1, scens)
-        def _(k):
-            ufull_copy(k).start()
+            @pl.loop(1, scens)
+            def _(k):
+                upart_wait(k)
+
+            @pl.loop(0, scens)
+            def _(k):
+                bpart_wait(k)
+
+            upper_full[pl.ds(pl.multiple_of(me_s * uchunk, 16), uchunk), :] = tree_sum(
+                [upper_gathered[i].astype(F32) for i in range(2 * scens)]
+            ).astype(BF16)
+
+            @pl.loop(1, scens)
+            def _(k):
+                ufull_copy(k).start()
 
     for at in range(0, TILE, PANEL):
         sweep_rows(matrix, at)
-        if at == 3 * PANEL:
+        if at == 2 * PANEL:
+            below_terms()
             upper_terms()
         if at == 6 * PANEL:
             upper_sum()
@@ -461,15 +556,46 @@
     def fetch(ref):
         return jnp.concatenate([ref[0:1, :], ref[1:2, :]], axis=1)
 
-    def vec_copy(step, side):
+    lane_count = 4
+    seam = scens == 16 and links == 16
+    lane = lax.rem(me_s, lane_count)
+    first_lane = me_s - lane
+
+    def at_seam(side):
+        return me_t == links // 2 - side if seam else me_t < 0
+
+    def vec_copy(step, side, extra):
+        cross = at_seam(side)
+        if extra:
+            target = first_lane + jnp.where(lane == 0, 2, 1)
+        else:
+            target = jnp.where(cross, first_lane + lane_count - 1 - lane, me_s)
+        slot = 2 * step + side
         return pltpu.make_async_remote_copy(
-            src_ref=vec_send.at[2 * step + side],
-            dst_ref=vec_recv.at[2 * step + side],
-            send_sem=vsend_sems.at[2 * step + side],
-            recv_sem=vrecv_sems.at[2 * step + side],
-            device_id={"link": link_source(1) if side == 0 else link_peer(1)},
-            device_id_type=MESH,
-        )
+            src_ref=vec_send.at[slot],
+            dst_ref=vec_recv.at[slot],
+            send_sem=vsend_sems.at[2 * slot + extra],
+            recv_sem=vrecv_sems.at[slot],
+            device_id={
+                "scen": target,
+                "link": link_source(1) if side == 0 else link_peer(1),
+            },
+            device_id_type=MESH,
+        )
+
+    def vec_act(step, side, act):
+        cross = at_seam(side)
+        edge = (lane == 0) | (lane == lane_count - 1)
+
+        @pl.when(jnp.logical_not(cross) | edge)
+        def _():
+            act(vec_copy(step, side, 0))
+
+        if seam:
+
+            @pl.when(cross & edge)
+            def _():
+                act(vec_copy(step, side, 1))
 
     colour = lax.rem(me_t, 2)
     vec_send[...] = jnp.zeros_like(vec_send)
@@ -479,9 +605,11 @@
     def _():
         current[...] = solve(right_side[...])
 
-    @pl.loop(1, scens)
-    def _(k):
-        ufull_wait(k)
+    @pl.when(me_t + 1 < links)
+    def _():
+        @pl.loop(1, scens)
+        def _(k):
+            ufull_wait(k)
 
     for step in range(2 * SWEEPS - 1):
 
@@ -490,27 +618,28 @@
             @pl.when(me_t > 0)
             def _():
                 put(vec_send.at[2 * step], current[...])
-                vec_copy(step, 0).start()
+                vec_act(step, 0, lambda copy: copy.start())
 
             @pl.when(me_t + 1 < links)
             def _():
                 put(vec_send.at[2 * step + 1], to_next(current[...]))
-                vec_copy(step, 1).start()
+                vec_act(step, 1, lambda copy: copy.start())
 
         @pl.when(colour != step % 2)
         def _():
+            current[...] = right_side[...]
+
             @pl.when(me_t + 1 < links)
             def _():
-                vec_copy(step, 0).wait_recv()
-
-            coupled = from_next(fetch(vec_recv.at[2 * step]))
+                vec_copy(step, 0, 0).wait_recv()
+                current[...] -= from_next(fetch(vec_recv.at[2 * step]))
 
             @pl.when(me_t > 0)
             def _():
-                vec_copy(step, 1).wait_recv()
-
-            coupled = coupled + fetch(vec_recv.at[2 * step + 1])
-            current[...] = solve(right_side[...] - coupled)
+                vec_copy(step, 1, 0).wait_recv()
+                current[...] -= fetch(vec_recv.at[2 * step + 1])
+
+            current[...] = solve(current[...])
 
     direction_out[...] = current[...]
 
@@ -565,12 +694,23 @@
     def _(k):
         part_copy(k).wait_send()
         full_copy(k).wait_send()
-        upart_copy(k).wait_send()
-        ufull_copy(k).wait_send()
+
+    @pl.when(me_t + 1 < links)
+    def _():
+        up_copy.wait_send()
+
+        @pl.loop(1, scens)
+        def _(k):
+            upart_copy(k).wait_send()
+            ufull_copy(k).wait_send()
 
     @pl.when(me_t > 0)
     def _():
-        next_copy.wait_send()
+        down_copy.wait_send()
+
+        @pl.loop(0, scens)
+        def _(k):
+            bpart_copy(k).wait_send()
 
     for step in range(2 * SWEEPS - 1):
 
@@ -578,11 +718,11 @@
         def _():
             @pl.when(me_t > 0)
             def _():
-                vec_copy(step, 0).wait_send()
+                vec_act(step, 0, lambda copy: copy.wait_send())
 
             @pl.when(me_t + 1 < links)
             def _():
-                vec_copy(step, 1).wait_send()
+                vec_act(step, 1, lambda copy: copy.wait_send())
 
     @pl.loop(1, links)
     def _(k):
@@ -620,10 +760,14 @@
             pltpu.VMEM((scens, 3 * HALF // scens, HALF), F32),
             pltpu.VMEM((3 * HALF, HALF), F32),
             pltpu.VMEM((TILE, TILE), F32),
-            pltpu.VMEM((width, TILE), BF16),
-            pltpu.VMEM((width, TILE), BF16),
+            pltpu.VMEM((TILE, width // 2), BF16),
+            pltpu.VMEM((TILE, width // 2), BF16),
+            pltpu.VMEM((TILE, width // 2), BF16),
+            pltpu.VMEM((width // 2, TILE), BF16),
+            pltpu.VMEM((width // 2, TILE), BF16),
             pltpu.VMEM((2 * TILE, HALF), BF16),
-            pltpu.VMEM((scens, 2 * TILE // scens, HALF), BF16),
+            pltpu.VMEM((2 * TILE, HALF), BF16),
+            pltpu.VMEM((2 * scens, 2 * TILE // scens, HALF), BF16),
             pltpu.VMEM((2 * TILE, HALF), BF16),
             pltpu.VMEM((1, TILE), F32),
             pltpu.VMEM((2 * steps, 8, HALF), F32),
@@ -637,13 +781,15 @@
             dma((scens,)),
             dma((scens,)),
             dma((scens,)),
-            dma,
-            dma,
-            dma((scens,)),
-            dma((scens,)),
-            dma((scens,)),
-            dma((scens,)),
-            dma((2 * steps,)),
+            dma((2,)),
+            dma((2,)),
+            dma((scens,)),
+            dma((scens,)),
+            dma((scens,)),
+            dma((scens,)),
+            dma((scens,)),
+            dma((scens,)),
+            dma((4 * steps,)),
             dma((2 * steps,)),
             dma((links,)),
             dma((links,)),

time: 100 us -> 86.2 us (0.86)
  Pallas kernels: 96.4 us -> 82.6 us
    pallas_call x1, Pallas kernels: 96.4 us -> 82.6 us  [shards(): pl.pallas_call(functools.partial(kernel, scens, links), out_shape=(jax.Sh...]
where the time goes in v2:
time: 86.2 us; the launch traced here: 86 us
  Pallas kernels  82.6 us (96%)
  local copies, waits for them, and re-layouts  2.77 us (3%)
    pallas_call x1, Pallas kernels, shards(): pl.pallas_call(functools.partial(kernel, scens, links), out_shape=(jax.Sh...  82.6 us
    unnamed x2, local copies, waits for them, and re-layouts  2.77 us

profile of v2, /device:TPU:1, one launch (start us, length us, event | category | flops | bytes accessed | tf_op | source)
XLA Modules:
  0.0 86.0 jit_solution(6507522175625034630)
XLA Ops:
  0.6 82.6 %coloured_sweeps.1 = (f32[1,256]{1,0:T(1,128)}, f32[162,128]{1,0:T(8,128)}) custom-call(s32[12,16]{1,0:T(8,128)} %ids_v.1, s32[12,16]{1,0:T(8,128)} %ids_v.1, bf16[12,2048,256]{2,1,0:T(8,128)(2,1)} %rows_hbm.1, f32[162,2048]{1,0:T(8,128)} %scaling_hbm.1, f32[1,256]{1,0:T(1,128)} %bitcast.3, f32[1,256]{1,0:T(1,128)} %bitcast.4), custom_call_target="tpu_custom_call" | custom-call | tf_op jit(solution)/shard_map/coloured_sweeps/pallas_call | solution.py:740
  83.3 1.2 %copy.9 = f32[256]{0:T(256)} copy(f32[256]{0:T(256)} %bitcast.5) | data formatting | bytes 2048
  84.5 1.5 %copy.10 = f32[162,128]{1,0:T(8,128)} copy(f32[162,128]{1,0:T(8,128)} %get-tuple-element.9) | data formatting | bytes 165888

commit v3 on v2

--- a/solution.py
+++ b/solution.py
@@ -9,6 +9,10 @@
 
 SWEEPS = 2
 HALF = 128
+AHEAD = 3
+PIECES = 8
+SEAM_TURN = 4
+FIRST, SECOND = 2, 4
 TILE = 256
 PANEL = 32
 HIGHEST = lax.Precision.HIGHEST
@@ -177,8 +181,12 @@
 
     scaling_copy = pltpu.make_async_copy(scaling_hbm, scaling, scaling_sem)
     scaling_copy.start()
-    for c in range(slots):
-        pltpu.make_async_copy(rows_hbm.at[c], rows.at[c], row_sems.at[c]).start()
+
+    def row_copy(c):
+        return pltpu.make_async_copy(rows_hbm.at[c], rows.at[c], row_sems.at[c])
+
+    for c in range(AHEAD):
+        row_copy(c).start()
 
     vec_recv[...] = jnp.zeros_like(vec_recv)
     barrier = pltpu.get_barrier_semaphore()
@@ -221,7 +229,6 @@
     names = lax.broadcasted_iota(jnp.int32, (slots, TILE), 1)
     for t in range(links):
         spread[t * 16 : t * 16 + slots, :] = (ids_v[:, t : t + 1] == names).astype(F32)
-    slot_send[...] = jnp.zeros_like(slot_send)
 
     def scale_row(name, keep):
         row = scaling[pl.ds(jnp.minimum(name, scen_count - 1), 1), :]
@@ -244,9 +251,13 @@
         total[...] += summed
 
     def arrived(c):
-        pltpu.make_async_copy(rows_hbm.at[c], rows.at[c], row_sems.at[c]).wait()
-
-    early = slots // 2
+        row_copy(c).wait()
+
+        @pl.when(c + AHEAD < slots)
+        def _():
+            row_copy(c + AHEAD).start()
+
+    early = slots - AHEAD
 
     @pl.loop(0, early)
     def _(c):
@@ -264,36 +275,59 @@
     for at in range(0, part_width, TILE):
         beyond = part_width + at
         block = rows[up_slot, beyond : beyond + TILE, :]
-        up_send[:, at : at + TILE] = (
-            block.T.astype(F32) * up_row[:, beyond : beyond + TILE]
-        ).astype(BF16)
+        scaled = (block.T.astype(F32) * up_row[:, beyond : beyond + TILE]).astype(BF16)
+        for inner in range(0, TILE, part_width // PIECES):
+            up_send[(at + inner) // (part_width // PIECES)] = scaled[
+                :, inner : inner + part_width // PIECES
+            ]
 
     pl.semaphore_wait(barrier, 3 * (scens - 1) + links - 1)
 
-    down_copy = pltpu.make_async_remote_copy(
-        src_ref=down_send,
-        dst_ref=down_got,
-        send_sem=down_sems.at[0],
-        recv_sem=down_sems.at[1],
-        device_id={"link": link_source(1)},
-        device_id_type=MESH,
-    )
-    up_copy = pltpu.make_async_remote_copy(
-        src_ref=up_send,
-        dst_ref=up_got,
-        send_sem=up_sems.at[0],
-        recv_sem=up_sems.at[1],
-        device_id={"link": link_peer(1)},
-        device_id_type=MESH,
-    )
-
-    @pl.when(me_t > 0)
+    piece = part_width // PIECES
+    seam = scens == 16 and links == 16
+
+    def at_seam(side):
+        return (me_t == links // 2 - side) if seam else (me_t < 0)
+
+    def row_pieces(side, at, count):
+        if side == 0:
+            span = pl.ds(at * piece, count * piece)
+            source, target = down_send.at[span], down_got.at[span]
+            sems, peer = down_sems, link_source(1)
+        else:
+            span = pl.ds(at, count)
+            source, target = up_send.at[span], up_got.at[span]
+            sems, peer = up_sems, link_peer(1)
+        return pltpu.make_async_remote_copy(
+            src_ref=source,
+            dst_ref=target,
+            send_sem=sems.at[0],
+            recv_sem=sems.at[1],
+            device_id={"link": peer},
+            device_id_type=MESH,
+        )
+
+    down_copy = row_pieces(0, 0, PIECES)
+    up_copy = row_pieces(1, 0, PIECES)
+
+    def seam_rows(first, last):
+        for side in range(2):
+
+            @pl.when(at_seam(side))
+            def _():
+                for at in range(first, last):
+                    row_pieces(side, at, 1).start()
+
+    @pl.when((me_t > 0) & jnp.logical_not(at_seam(0)))
     def _():
         down_copy.start()
 
-    @pl.when(me_t + 1 < links)
+    @pl.when((me_t + 1 < links) & jnp.logical_not(at_seam(1)))
     def _():
         up_copy.start()
+
+    if seam:
+        seam_rows(0, FIRST)
 
     for at in range(0, part_width, TILE):
         block = rows[up_slot, at : at + TILE, :]
@@ -426,6 +460,9 @@
     def _(k):
         part_copy(k).start()
 
+    if seam:
+        seam_rows(FIRST, SECOND)
+
     gathered[me_s] = part[pl.ds(pl.multiple_of(me_s * chunk, 8), chunk), :]
 
     @pl.loop(1, scens)
@@ -439,6 +476,9 @@
     @pl.loop(1, scens)
     def _(k):
         full_copy(k).start()
+
+    if seam:
+        seam_rows(SECOND, PIECES)
 
     @pl.loop(1, scens)
     def _(k):
@@ -462,11 +502,10 @@
         @pl.when(me_t > 0)
         def _():
             up_copy.wait_recv()
+            scaled = jnp.concatenate([up_got[i] for i in range(PIECES)], axis=1)
             store_wide(
                 below_part,
-                jnp.dot(
-                    up_got[...], rows[down_slot, part_width:, :], preferred_element_type=F32
-                ),
+                jnp.dot(scaled, rows[down_slot, part_width:, :], preferred_element_type=F32),
             )
 
             @pl.loop(0, scens)
@@ -511,11 +550,15 @@
 
     for at in range(0, TILE, PANEL):
         sweep_rows(matrix, at)
-        if at == 2 * PANEL:
-            below_terms()
-            upper_terms()
-        if at == 6 * PANEL:
-            upper_sum()
+        for turn, late in ((0, False), (SEAM_TURN, True)):
+            if at == turn * PANEL and (seam or not late):
+                pl.when(at_seam(0) == late)(below_terms)
+                pl.when(at_seam(1) == late)(upper_terms)
+        if at == 4 * PANEL:
+            pl.when(jnp.logical_not(at_seam(1)))(upper_sum)
+
+    if seam:
+        pl.when(at_seam(1))(upper_sum)
 
     def solve(vector):
         wide = jnp.broadcast_to(vector, (8, TILE))
@@ -557,12 +600,8 @@
         return jnp.concatenate([ref[0:1, :], ref[1:2, :]], axis=1)
 
     lane_count = 4
-    seam = scens == 16 and links == 16
     lane = lax.rem(me_s, lane_count)
     first_lane = me_s - lane
-
-    def at_seam(side):
-        return me_t == links // 2 - side if seam else me_t < 0
 
     def vec_copy(step, side, extra):
         cross = at_seam(side)
@@ -643,21 +682,22 @@
 
     direction_out[...] = current[...]
 
-    half = jnp.broadcast_to(current[...].astype(BF16), (16, TILE))
-
-    @pl.loop(0, slots)
-    def _(c):
-        for j in range(links):
-            value = lax.dot_general(
-                half,
-                rows[c, j * pieces : (j + 1) * pieces, :],
-                (((1,), (1,)), ((), ())),
-                preferred_element_type=F32,
-            )
-            slot_send[j, pl.ds(c, 1), :] = value[:1, :]
+    rounded = current[...].astype(BF16)
+    half = jnp.broadcast_to(rounded, (16, TILE))
+    direct = rounded.astype(F32)
+
+    def slot_order(k):
+        if not seam:
+            return lax.rem(me_t + k + 1, links)
+        block = links // 2
+        near = jnp.where(k < 12, k - 4, jnp.where(k < 15, k - 11, 0))
+        turn = jnp.where(k < block, k, near)
+        side = me_t // block
+        side = jnp.where(k < block, 1 - side, side)
+        return side * block + lax.rem(me_t + turn, block)
 
     def slot_copy(k):
-        peer = link_peer(k)
+        peer = slot_order(k)
         return pltpu.make_async_remote_copy(
             src_ref=slot_send.at[peer],
             dst_ref=slot_recv.at[me_t],
@@ -667,9 +707,28 @@
             device_id_type=MESH,
         )
 
-    @pl.loop(1, links)
-    def _(k):
-        slot_copy(k).start()
+    @pl.loop(0, links)
+    def _(k):
+        peer = slot_order(k)
+        at = pl.ds(pl.multiple_of(peer * pieces, HALF), pieces)
+        values = []
+        for c in range(slots):
+            block = rows[c, at, :]
+            if c % 2:
+                value = block.astype(F32) * direct
+                value = value[:, :HALF] + value[:, HALF:]
+                values.append(jnp.sum(value.T, axis=0, keepdims=True))
+            else:
+                value = lax.dot_general(
+                    half, block, (((1,), (1,)), ((), ())), preferred_element_type=F32
+                )
+                values.append(value[:1, :])
+        values.append(jnp.zeros((16 - slots, pieces), F32))
+        slot_send[peer] = jnp.concatenate(values, axis=0)
+
+        @pl.when(k + 1 < links)
+        def _():
+            slot_copy(k).start()
 
     slot_recv[me_t] = slot_send[me_t]
 
@@ -724,9 +783,14 @@
             def _():
                 vec_act(step, 1, lambda copy: copy.wait_send())
 
-    @pl.loop(1, links)
+    @pl.loop(0, links - 1)
     def _(k):
         slot_copy(k).wait_send()
+
+
+def hand_over(direction, step, direction_out, step_out):
+    direction_out[...] = direction[...]
+    step_out[...] = step[...]
 
 
 def shards(link_rows, slot_scenario, diag_scaling, regulariser, right_side):
@@ -740,8 +804,8 @@
     direction, step = pl.pallas_call(
         functools.partial(kernel, scens, links),
         out_shape=(
-            jax.ShapeDtypeStruct((1, TILE), F32),
-            jax.ShapeDtypeStruct((scen_count, pieces), F32),
+            pltpu.VMEM((1, TILE), F32),
+            pltpu.VMEM((scen_count, pieces), F32),
         ),
         in_specs=[
             pl.BlockSpec(memory_space=pltpu.SMEM),
@@ -761,8 +825,8 @@
             pltpu.VMEM((3 * HALF, HALF), F32),
             pltpu.VMEM((TILE, TILE), F32),
             pltpu.VMEM((TILE, width // 2), BF16),
-            pltpu.VMEM((TILE, width // 2), BF16),
-            pltpu.VMEM((TILE, width // 2), BF16),
+            pltpu.VMEM((PIECES, TILE, width // 2 // PIECES), BF16),
+            pltpu.VMEM((PIECES, TILE, width // 2 // PIECES), BF16),
             pltpu.VMEM((width // 2, TILE), BF16),
             pltpu.VMEM((width // 2, TILE), BF16),
             pltpu.VMEM((2 * TILE, HALF), BF16),
@@ -806,6 +870,17 @@
         regulariser.reshape(1, TILE),
         right_side.reshape(1, TILE),
     )
+    direction, step = pl.pallas_call(
+        hand_over,
+        out_shape=(
+            jax.ShapeDtypeStruct((1, TILE), F32),
+            jax.ShapeDtypeStruct((scen_count, pieces), F32),
+        ),
+        in_specs=[vmem, vmem],
+        out_specs=(vmem, vmem),
+        compiler_params=pltpu.CompilerParams(vmem_limit_bytes=2**20),
+        name="hand_over",
+    )(direction, step)
     return direction.reshape(TILE), step
 
 

time: 86.2 us -> 74.9 us (0.87)
  Pallas kernels: 82.6 us -> 74.1 us
  local copies, waits for them, and re-layouts: 2.77 us -> 0 us
    pallas_call x1 -> x2, Pallas kernels: 82.6 us -> 74.1 us  [the longest x1 73.5 us: shards(): pl.pallas_call(functools.partial(kernel, scens, links), out_shape=(pltpu....]
    unnamed x2 -> x0, local copies, waits for them, and re-layouts: 2.77 us -> none
where the time goes in v3:
time: 74.9 us; the launch traced here: 74.7 us
  Pallas kernels  74.1 us (99%)
    pallas_call x1, Pallas kernels, shards(): pl.pallas_call(functools.partial(kernel, scens, links), out_shape=(pltpu....  73.5 us

profile of v3, /device:TPU:1, one launch (start us, length us, event | category | flops | bytes accessed | tf_op | source)
XLA Modules:
  0.0 74.7 jit_solution(8621025727620616121)
XLA Ops:
  0.6 73.5 %coloured_sweeps.1 = (f32[1,256]{1,0:T(1,128)S(1)}, f32[162,128]{1,0:T(8,128)S(1)}) custom-call(s32[12,16]{1,0:T(8,128)} %ids_v.1, s32[12,16]{1,0:T(8,128)} %ids_v.1, bf16[12,2048,256]{2,1,0:T(8,128)(2,1)} %rows_hbm.1, f32[162,2048]{1,0:T(8,128)} %scaling_hbm.1, f32[1,256]{1,0:T(1,128)} %bitcast.3, f32[1,256]{1,0:T(1,128)} %bitcast.4), custom_call_target="tpu_custom_call" | custom-call | tf_op jit(solution)/shard_map/coloured_sweeps/pallas_call | solution.py:804
  74.1 0.6 hand_over.1

commit v4 on v3

--- a/solution.py
+++ b/solution.py
@@ -11,7 +11,7 @@
 HALF = 128
 AHEAD = 3
 PIECES = 8
-SEAM_TURN = 4
+BELOW_TURN, UPPER_TURN = 2, 4
 FIRST, SECOND = 2, 4
 TILE = 256
 PANEL = 32
@@ -550,10 +550,14 @@
 
     for at in range(0, TILE, PANEL):
         sweep_rows(matrix, at)
-        for turn, late in ((0, False), (SEAM_TURN, True)):
-            if at == turn * PANEL and (seam or not late):
-                pl.when(at_seam(0) == late)(below_terms)
-                pl.when(at_seam(1) == late)(upper_terms)
+        turn = at // PANEL
+        if turn == 0:
+            pl.when(jnp.logical_not(at_seam(0)))(below_terms)
+            pl.when(jnp.logical_not(at_seam(1)))(upper_terms)
+        if seam and turn == BELOW_TURN:
+            pl.when(at_seam(0))(below_terms)
+        if seam and turn == UPPER_TURN:
+            pl.when(at_seam(1))(upper_terms)
         if at == 4 * PANEL:
             pl.when(jnp.logical_not(at_seam(1)))(upper_sum)
 

time: 74.9 us -> 72.9 us (0.973)
  Pallas kernels: 74.1 us -> 72.1 us
    pallas_call x1, Pallas kernels: 73.5 us -> 71.5 us  [shards(): pl.pallas_call(functools.partial(kernel, scens, links), out_shape=(pltpu....]
where the time goes in v4:
time: 72.9 us; the launch traced here: 72.8 us
  Pallas kernels  72.1 us (99%)
    pallas_call x1, Pallas kernels, shards(): pl.pallas_call(functools.partial(kernel, scens, links), out_shape=(pltpu....  71.5 us

profile of v4, /device:TPU:1, one launch (start us, length us, event | category | flops | bytes accessed | tf_op | source)
XLA Modules:
  0.0 72.8 jit_solution(3389843297249078258)
XLA Ops:
  0.6 71.5 %coloured_sweeps.1 = (f32[1,256]{1,0:T(1,128)S(1)}, f32[162,128]{1,0:T(8,128)S(1)}) custom-call(s32[12,16]{1,0:T(8,128)} %ids_v.1, s32[12,16]{1,0:T(8,128)} %ids_v.1, bf16[12,2048,256]{2,1,0:T(8,128)(2,1)} %rows_hbm.1, f32[162,2048]{1,0:T(8,128)} %scaling_hbm.1, f32[1,256]{1,0:T(1,128)} %bitcast.3, f32[1,256]{1,0:T(1,128)} %bitcast.4), custom_call_target="tpu_custom_call" | custom-call | tf_op jit(solution)/shard_map/coloured_sweeps/pallas_call | solution.py:808
  72.1 0.6 hand_over.1

commit v5 on v4

--- a/solution.py
+++ b/solution.py
@@ -170,9 +170,6 @@
     def scen_peer(k):
         return lax.rem(me_s + k, scens)
 
-    def scen_source(k):
-        return lax.rem(me_s + scens - k, scens)
-
     def link_peer(k):
         return lax.rem(me_t + k, links)
 
@@ -349,112 +346,73 @@
         return pltpu.make_async_remote_copy(
             src_ref=part.at[pl.ds(pl.multiple_of(peer * chunk, 8), chunk)],
             dst_ref=gathered.at[me_s],
-            send_sem=part_send.at[k],
-            recv_sem=part_recv.at[me_s],
+            send_sem=part_send,
+            recv_sem=part_recv,
             device_id={"scen": peer},
             device_id_type=MESH,
         )
 
-    def part_wait(k):
-        source = scen_source(k)
-        pltpu.make_async_remote_copy(
-            src_ref=part.at[pl.ds(0, chunk)],
-            dst_ref=gathered.at[source],
-            send_sem=part_send.at[k],
-            recv_sem=part_recv.at[source],
-            device_id={"scen": source},
+    def whole(ref, send_sem, recv_sem):
+        return pltpu.make_async_remote_copy(
+            src_ref=ref,
+            dst_ref=ref,
+            send_sem=send_sem,
+            recv_sem=recv_sem,
+            device_id={"scen": scen_peer(1)},
             device_id_type=MESH,
-        ).wait_recv()
+        )
+
+    others = scens - 1
+    part_all = whole(part.at[pl.ds(0, others * chunk)], part_send, part_recv)
+    full_all = whole(full.at[pl.ds(0, others * chunk)], full_send, full_recv)
+    upart_all = whole(upper_part.at[pl.ds(0, others * uchunk)], upart_send, upart_recv)
+    bpart_all = whole(below_part, bpart_send, bpart_recv)
+    ufull_all = whole(upper_full.at[pl.ds(0, others * uchunk)], ufull_send, ufull_recv)
+    slot_all = whole(slot_send.at[pl.ds(0, links - 1)], slot_send_sems, slot_recv_sems)
 
     def full_copy(k):
         mine = pl.ds(pl.multiple_of(me_s * chunk, 8), chunk)
         return pltpu.make_async_remote_copy(
             src_ref=full.at[mine],
             dst_ref=full.at[mine],
-            send_sem=full_send.at[k],
-            recv_sem=full_recv.at[me_s],
+            send_sem=full_send,
+            recv_sem=full_recv,
             device_id={"scen": scen_peer(k)},
             device_id_type=MESH,
         )
-
-    def full_wait(k):
-        source = scen_source(k)
-        theirs = pl.ds(pl.multiple_of(source * chunk, 8), chunk)
-        pltpu.make_async_remote_copy(
-            src_ref=full.at[theirs],
-            dst_ref=full.at[theirs],
-            send_sem=full_send.at[k],
-            recv_sem=full_recv.at[source],
-            device_id={"scen": source},
-            device_id_type=MESH,
-        ).wait_recv()
 
     def upart_copy(k):
         peer = scen_peer(k)
         return pltpu.make_async_remote_copy(
             src_ref=upper_part.at[pl.ds(pl.multiple_of(peer * uchunk, 16), uchunk)],
             dst_ref=upper_gathered.at[me_s],
-            send_sem=upart_send.at[k],
-            recv_sem=upart_recv.at[me_s],
+            send_sem=upart_send,
+            recv_sem=upart_recv,
             device_id={"scen": peer},
             device_id_type=MESH,
         )
-
-    def upart_wait(k):
-        source = scen_source(k)
-        pltpu.make_async_remote_copy(
-            src_ref=upper_part.at[pl.ds(0, uchunk)],
-            dst_ref=upper_gathered.at[source],
-            send_sem=upart_send.at[k],
-            recv_sem=upart_recv.at[source],
-            device_id={"scen": source},
-            device_id_type=MESH,
-        ).wait_recv()
 
     def bpart_copy(k):
         peer = scen_peer(k)
         return pltpu.make_async_remote_copy(
             src_ref=below_part.at[pl.ds(pl.multiple_of(peer * uchunk, 16), uchunk)],
             dst_ref=upper_gathered.at[scens + me_s],
-            send_sem=bpart_send.at[k],
-            recv_sem=bpart_recv.at[me_s],
+            send_sem=bpart_send,
+            recv_sem=bpart_recv,
             device_id={"scen": peer, "link": link_source(1)},
             device_id_type=MESH,
         )
-
-    def bpart_wait(k):
-        source = scen_source(k)
-        pltpu.make_async_remote_copy(
-            src_ref=below_part.at[pl.ds(0, uchunk)],
-            dst_ref=upper_gathered.at[scens + source],
-            send_sem=bpart_send.at[k],
-            recv_sem=bpart_recv.at[source],
-            device_id={"scen": source, "link": link_peer(1)},
-            device_id_type=MESH,
-        ).wait_recv()
 
     def ufull_copy(k):
         mine = pl.ds(pl.multiple_of(me_s * uchunk, 16), uchunk)
         return pltpu.make_async_remote_copy(
             src_ref=upper_full.at[mine],
             dst_ref=upper_full.at[mine],
-            send_sem=ufull_send.at[k],
-            recv_sem=ufull_recv.at[me_s],
+            send_sem=ufull_send,
+            recv_sem=ufull_recv,
             device_id={"scen": scen_peer(k)},
             device_id_type=MESH,
         )
-
-    def ufull_wait(k):
-        source = scen_source(k)
-        theirs = pl.ds(pl.multiple_of(source * uchunk, 16), uchunk)
-        pltpu.make_async_remote_copy(
-            src_ref=upper_full.at[theirs],
-            dst_ref=upper_full.at[theirs],
-            send_sem=ufull_send.at[k],
-            recv_sem=ufull_recv.at[source],
-            device_id={"scen": source},
-            device_id_type=MESH,
-        ).wait_recv()
 
     @pl.loop(1, scens)
     def _(k):
@@ -465,9 +423,7 @@
 
     gathered[me_s] = part[pl.ds(pl.multiple_of(me_s * chunk, 8), chunk), :]
 
-    @pl.loop(1, scens)
-    def _(k):
-        part_wait(k)
+    part_all.wait_recv()
 
     full[pl.ds(pl.multiple_of(me_s * chunk, 8), chunk), :] = tree_sum(
         [gathered[i] for i in range(scens)]
@@ -480,9 +436,7 @@
     if seam:
         seam_rows(SECOND, PIECES)
 
-    @pl.loop(1, scens)
-    def _(k):
-        full_wait(k)
+    full_all.wait_recv()
 
     corner = full[HALF : 2 * HALF, :]
     matrix[:HALF, :HALF] = full[:HALF, :]
@@ -532,13 +486,8 @@
     def upper_sum():
         @pl.when(me_t + 1 < links)
         def _():
-            @pl.loop(1, scens)
-            def _(k):
-                upart_wait(k)
-
-            @pl.loop(0, scens)
-            def _(k):
-                bpart_wait(k)
+            upart_all.wait_recv()
+            bpart_all.wait_recv()
 
             upper_full[pl.ds(pl.multiple_of(me_s * uchunk, 16), uchunk), :] = tree_sum(
                 [upper_gathered[i].astype(F32) for i in range(2 * scens)]
@@ -650,9 +599,7 @@
 
     @pl.when(me_t + 1 < links)
     def _():
-        @pl.loop(1, scens)
-        def _(k):
-            ufull_wait(k)
+        ufull_all.wait_recv()
 
     for step in range(2 * SWEEPS - 1):
 
@@ -705,8 +652,8 @@
         return pltpu.make_async_remote_copy(
             src_ref=slot_send.at[peer],
             dst_ref=slot_recv.at[me_t],
-            send_sem=slot_send_sems.at[k],
-            recv_sem=slot_recv_sems.at[me_t],
+            send_sem=slot_send_sems,
+            recv_sem=slot_recv_sems,
             device_id={"link": peer},
             device_id_type=MESH,
         )
@@ -736,44 +683,28 @@
 
     slot_recv[me_t] = slot_send[me_t]
 
-    @pl.loop(1, links)
-    def _(k):
-        source = link_source(k)
-        pltpu.make_async_remote_copy(
-            src_ref=slot_send.at[source],
-            dst_ref=slot_recv.at[source],
-            send_sem=slot_send_sems.at[k],
-            recv_sem=slot_recv_sems.at[source],
-            device_id={"link": source},
-            device_id_type=MESH,
-        ).wait_recv()
+    slot_all.wait_recv()
 
     values = slot_recv[...].reshape(links * 16, pieces)
     summed = dot_tt(spread[...], values)
     columns = scaling[:, pl.ds(pl.multiple_of(me_t * pieces, HALF), pieces)]
     step_out[...] = columns * summed[:scen_count, :]
 
-    @pl.loop(1, scens)
-    def _(k):
-        part_copy(k).wait_send()
-        full_copy(k).wait_send()
+    part_all.wait_send()
+    full_all.wait_send()
 
     @pl.when(me_t + 1 < links)
     def _():
         up_copy.wait_send()
 
-        @pl.loop(1, scens)
-        def _(k):
-            upart_copy(k).wait_send()
-            ufull_copy(k).wait_send()
+        upart_all.wait_send()
+        ufull_all.wait_send()
 
     @pl.when(me_t > 0)
     def _():
         down_copy.wait_send()
 
-        @pl.loop(0, scens)
-        def _(k):
-            bpart_copy(k).wait_send()
+        bpart_all.wait_send()
 
     for step in range(2 * SWEEPS - 1):
 
@@ -787,9 +718,7 @@
             def _():
                 vec_act(step, 1, lambda copy: copy.wait_send())
 
-    @pl.loop(0, links - 1)
-    def _(k):
-        slot_copy(k).wait_send()
+    slot_all.wait_send()
 
 
 def hand_over(direction, step, direction_out, step_out):
@@ -845,22 +774,22 @@
             pltpu.VMEM((links, 16, pieces), F32),
             dma((slots,)),
             dma,
-            dma((scens,)),
-            dma((scens,)),
-            dma((scens,)),
-            dma((scens,)),
+            dma,
+            dma,
+            dma,
+            dma,
             dma((2,)),
             dma((2,)),
-            dma((scens,)),
-            dma((scens,)),
-            dma((scens,)),
-            dma((scens,)),
-            dma((scens,)),
-            dma((scens,)),
+            dma,
+            dma,
+            dma,
+            dma,
+            dma,
+            dma,
             dma((4 * steps,)),
             dma((2 * steps,)),
-            dma((links,)),
-            dma((links,)),
+            dma,
+            dma,
         ],
         compiler_params=pltpu.CompilerParams(
             collective_id=0, has_side_effects=True, vmem_limit_bytes=56 * 2**20

time: 72.9 us -> 70.5 us (0.967)
  Pallas kernels: 72.1 us -> 69.7 us
    pallas_call x1, Pallas kernels: 71.5 us -> 69 us  [shards(): pl.pallas_call(functools.partial(kernel, scens, links), out_shape=(pltpu....]
where the time goes in v5:
time: 70.5 us; the launch traced here: 70.3 us
  Pallas kernels  69.7 us (99%)
    pallas_call x1, Pallas kernels, shards(): pl.pallas_call(functools.partial(kernel, scens, links), out_shape=(pltpu....  69 us

profile of v5, /device:TPU:1, one launch (start us, length us, event | category | flops | bytes accessed | tf_op | source)
XLA Modules:
  0.0 70.3 jit_solution(9045023475561435329)
XLA Ops:
  0.6 69.0 %coloured_sweeps.1 = (f32[1,256]{1,0:T(1,128)S(1)}, f32[162,128]{1,0:T(8,128)S(1)}) custom-call(s32[12,16]{1,0:T(8,128)} %ids_v.1, s32[12,16]{1,0:T(8,128)} %ids_v.1, bf16[12,2048,256]{2,1,0:T(8,128)(2,1)} %rows_hbm.1, f32[162,2048]{1,0:T(8,128)} %scaling_hbm.1, f32[1,256]{1,0:T(1,128)} %bitcast.3, f32[1,256]{1,0:T(1,128)} %bitcast.4), custom_call_target="tpu_custom_call" | custom-call | tf_op jit(solution)/shard_map/coloured_sweeps/pallas_call | solution.py:737
  69.7 0.6 hand_over.1
